TPU v7x, 256 devices: a whole 4x4x8 slice. The times are simulated.
256 devices in a mesh: frame: 64 (over y, z, core), head: 4 (over x).
Axes of the slice: x: 4, y: 4, z: 8, core: 2. Of those that a mesh axis runs over, the one named last changes fastest.
Arguments:
- span_q: bfloat16 [32768, 3072], P(('frame', 'head')), may hold values from -40 to 40
- span_k: bfloat16 [32768, 3072], P(('frame', 'head')), may hold values from -4 to 4
- span_v: bfloat16 [32768, 3072], P(('frame', 'head')), may hold values from -12 to 12
- bank_k: bfloat16 [1536, 32, 3072], P('frame', None, 'head'), may hold values from -4 to 4
- bank_v: bfloat16 [1536, 32, 3072], P('frame', None, 'head'), may hold values from -12 to 12
- frame_slot: int32 [1536], replicated, may hold values from 0 to 1535, as said below
- picks: int32 [64, 64], replicated, may hold values from 0 to 1535, as said below
- counts: int32 [64], replicated, may hold values from 44 to 64, as said below
- out_weight: bfloat16 [3072, 3072], P('head'), may hold values from -0.109375 to 0.109375
Outputs:
- mixed: bfloat16 [32768, 3072], P(('frame', 'head'))
Inputs may be any that keep to these rules, and one draw needn't show every extreme that they name: `frame_slot`: A permutation of the frame ids. For every span c the first counts[c] entries of picks[c] are distinct frames; at most 2 of them lie in bank rows j * 24 to (j + 1) * 24 - 1 for any j, and for every span some j holds exactly 2. Entries past counts[c] are frame ids that are not used. `counts`: some span retrieves exactly 64 frames.
All inputs are finite; a program needn't handle non-finite values.
Results may differ from a plain program's by a relative error of at most 0.013.
Values may be sent and summed in bfloat16 or wider, within the bound.
A program may use at most 128 MiB of HBM per device.

v0:
```python
import math

import jax
import jax.numpy as jnp
from jax import lax
from jax.sharding import PartitionSpec as P

HEAD_DIM = 128


def softmax_parts(scores, mask):
    return jnp.where(mask[None, :], scores, -1e30)


def head_cols(matrix, column):
    return lax.dynamic_slice_in_dim(matrix, column, HEAD_DIM, 1)


def local(span_q, span_k, span_v, bank_k, bank_v, frame_slot, picks, counts, out_weight):
    frames_count = lax.axis_size("frame")
    self_index = lax.axis_index("frame")
    longest = picks.shape[1]
    per_device = bank_k.shape[0]
    tokens_frame = bank_k.shape[1]
    width_here = bank_k.shape[2]
    capacity = (longest + frames_count - 1) // frames_count + 1
    total_frames = frame_slot.shape[0]
    heads_here = width_here // HEAD_DIM
    scale = 1.0 / math.sqrt(HEAD_DIM)
    table = jnp.arange(total_frames, dtype=jnp.int32)
    hits = picks[:, :, None] == table[None, None, :]
    bank_rows = jnp.sum(jnp.where(hits, frame_slot[None, None, :], 0), axis=2)
    position = jnp.arange(longest, dtype=jnp.int32)
    live = position[None, :] < counts[:, None]
    owners = bank_rows // per_device
    local_rows = bank_rows % per_device
    mine = live & (owners == self_index)
    ranking = jnp.cumsum(mine.astype(jnp.int32), axis=1) - 1
    levels = jnp.arange(capacity, dtype=jnp.int32)
    pick_one = mine[:, None, :] & (ranking[:, None, :] == levels[None, :, None])
    slot_row = jnp.sum(jnp.where(pick_one, local_rows[:, None, :], 0), axis=2)
    filled = jnp.any(pick_one, axis=2)[:, :, None, None]
    send_keys = jnp.where(filled, bank_k[slot_row], jnp.zeros((), bank_k.dtype))
    send_values = jnp.where(filled, bank_v[slot_row], jnp.zeros((), bank_v.dtype))
    queries, own_keys, own_values = (
        lax.all_to_all(span_q, "head", split_axis=1, concat_axis=0, tiled=True),
        lax.all_to_all(span_k, "head", split_axis=1, concat_axis=0, tiled=True),
        lax.all_to_all(span_v, "head", split_axis=1, concat_axis=0, tiled=True),
    )
    recv_keys, recv_values = (
        lax.all_to_all(send_keys, "frame", split_axis=0, concat_axis=0, tiled=True),
        lax.all_to_all(send_values, "frame", split_axis=0, concat_axis=0, tiled=True),
    )
    own_owner = lax.dynamic_slice_in_dim(owners, self_index, 1, 0)[0]
    own_live = lax.dynamic_slice_in_dim(live, self_index, 1, 0)[0]
    earlier = (
        (position[None, :] < position[:, None])
        & (own_owner[None, :] == own_owner[:, None])
        & own_live[None, :]
    )
    level_here = jnp.sum(earlier.astype(jnp.int32), axis=1)
    flat_slot = jnp.where(own_live, own_owner * capacity + level_here, 0)
    mem_keys = recv_keys.reshape(frames_count * capacity, tokens_frame, width_here)[flat_slot]
    mem_values = recv_values.reshape(frames_count * capacity, tokens_frame, width_here)[flat_slot]
    mem_keys = mem_keys.reshape(longest * tokens_frame, width_here)
    mem_values = mem_values.reshape(longest * tokens_frame, width_here)
    mem_live = jnp.repeat(own_live, tokens_frame)
    span_rows = queries.shape[0]
    block_rows = min(512, span_rows)
    blocks = span_rows // block_rows
    all_keys = jnp.concatenate([own_keys, mem_keys], axis=0)
    all_values = jnp.concatenate([own_values, mem_values], axis=0)
    all_live = jnp.concatenate([jnp.ones((span_rows,), bool), mem_live])

    def attend(query_block, column):
        scores = (
            jnp.einsum(
                "qd,kd->qk",
                query_block,
                head_cols(all_keys, column),
                preferred_element_type=jnp.float32,
            )
            * scale
        )
        scores = softmax_parts(scores, all_live)
        top = jnp.max(scores, axis=-1, keepdims=True)
        expo = jnp.exp(scores - top)
        total = jnp.sum(expo, axis=-1, keepdims=True)
        numer = jnp.dot(
            expo.astype(jnp.bfloat16),
            head_cols(all_values, column),
            preferred_element_type=jnp.float32,
        )
        return (numer / total).astype(jnp.bfloat16)

    def attend_step(item, attn_now):
        row_start = item % blocks * block_rows
        column = item // blocks * HEAD_DIM
        query_block = lax.dynamic_slice(queries, (row_start, column), (block_rows, HEAD_DIM))
        return lax.dynamic_update_slice(attn_now, attend(query_block, column), (row_start, column))

    attn = lax.fori_loop(
        0, heads_here * blocks, attend_step, jnp.zeros((span_rows, width_here), jnp.bfloat16)
    )
    return lax.psum_scatter(
        jnp.dot(attn, out_weight, preferred_element_type=jnp.float32).astype(jnp.bfloat16),
        "head",
        scatter_dimension=0,
        tiled=True,
    )


def solution(mesh):
    placed = (
        P(("frame", "head"), None),
        P(("frame", "head"), None),
        P(("frame", "head"), None),
        P("frame", None, "head"),
        P("frame", None, "head"),
        P(),
        P(),
        P(),
        P("head", None),
    )
    return jax.shard_map(
        local, mesh=mesh, in_specs=placed, out_specs=P(("frame", "head"), None), check_vma=False
    )
```

profile of v0, /device:TPU:1, one launch (start us, length us, event | category | flops | bytes accessed | tf_op | source)
XLA Modules:
  0.0 443.2 jit_solution(15052282341852663108)
XLA Ops:
  6.5 2.2 copy.29
  8.7 4.8 %all-to-all-start.3 = ((bf16[128,4,768]{2,0,1:T(8,128)(2,1)}), bf16[128,4,768]{2,0,1:T(8,128)(2,1)S(1)}, u32[]{:S(2)}, u32[]{:S(2)}) async-start(bf16[128,4,768]{2,0,1:T(8,128)(2,1)} %bitcast.52), calls=%async_computation.3 | async-start | bytes 1572864 | tf_op jit(solution)/shard_map/all_to_all | solution.py:48
  13.5 4.6 %select_reduce_fusion = s32[64,64]{1,0:T(8,128)S(1)} fusion(s32[1536]{0:T(1024)} %param.16, s32[64,64]{1,0:T(8,128)} %param.17), kind=kLoop, calls=%fused_computation.18 | loop fusion | flops 18870272 | bytes 38912 | tf_op jit(solution)/shard_map/reduce_sum | solution.py:32
  18.1 0.7 fusion.27
  18.8 0.2 reduce_window_sum.11
  19.1 0.1 select_reduce_fusion.1
  19.2 0.1 copy.21
  19.3 0.1 reshape.156
  19.5 3.6 gather_fusion.2
  23.1 3.6 gather_fusion
  26.7 0.1 fusion.20
  26.8 0.1 copy.20
  26.9 0.9 copy.30
  27.9 4.2 all-to-all-start.1
  32.1 10.0 %broadcast_select_fusion = (bf16[64,2,32,768]{3,2,1,0:T(8,128)(2,1)}, bf16[64,2,32,768]{3,2,1,0:T(8,128)(2,1)}) fusion(bf16[64,2,32,768]{3,2,1,0:T(8,128)(2,1)} %bitcast.55, pred[64,2]{1,0:T(8,128)(4,1)S(1)} %copy.20, bf16[64,2,32,768]{3,2,1,0:T(8,128)(2,1)} %bitcast.56), kind=kLoop, calls=%fused_computation.20 | loop fusion | flops 6291456 | bytes 25165952 | tf_op jit(solution)/shard_map/jit(_where)/select_n | solution.py:44
  42.1 156.2 %all_to_all.67 = bf16[64,2,32,768]{3,2,1,0:T(8,128)(2,1)} all-to-all(bf16[64,2,32,768]{3,2,1,0:T(8,128)(2,1)} %get-tuple-element.179), channel_id=1, replica_groups=mesh['frame'=64,'head'=4] {'frame'}, dimensions={0} | all-to-all | bytes 12582912 | tf_op jit(solution)/shard_map/all_to_all | solution.py:52
  198.2 6.1 %all-to-all-start.2 = ((bf16[64,2,32,768]{3,2,1,0:T(8,128)(2,1)}), bf16[64,2,32,768]{3,2,1,0:T(8,128)(2,1)}, u32[]{:S(2)}, u32[]{:S(2)}) async-start(bf16[64,2,32,768]{3,2,1,0:T(8,128)(2,1)} %get-tuple-element.180), calls=%async_computation.2 | async-start | bytes 12582912 | tf_op jit(solution)/shard_map/all_to_all | solution.py:51
  204.4 0.1 reshape.149
  204.5 0.9 copy.31
  205.5 0.2 convert_reduce_fusion
  205.7 5.2 %gather_fusion.3 = bf16[64,32,768]{2,1,0:T(8,128)(2,1)} fusion(bf16[128,32,768]{2,1,0:T(8,128)(2,1)} %bitcast.57, s32[1024]{0:T(1024)S(1)} %pad_clamp_fusion), kind=kCustom, calls=%fused_computation.3 | custom fusion | bytes 6291712 | tf_op jit(solution)/shard_map/gather | solution.py:64
  210.9 134.3 %all-to-all-done.2 = bf16[64,2,32,768]{3,2,1,0:T(8,128)(2,1)} async-done(((bf16[64,2,32,768]{3,2,1,0:T(8,128)(2,1)}), bf16[64,2,32,768]{3,2,1,0:T(8,128)(2,1)}, u32[]{:S(2)}, u32[]{:S(2)}) %all-to-all-start.2) | async-done | bytes 6291488 | tf_op jit(solution)/shard_map/all_to_all | solution.py:51
  345.2 3.5 all-to-all-start
  348.7 0.2 reduce-scatter.2.cloned.1.call-start
  348.9 4.0 pad_maximum_fusion.1
  353.0 5.2 %gather_fusion.1 = bf16[64,32,768]{2,1,0:T(8,128)(2,1)} fusion(bf16[128,32,768]{2,1,0:T(8,128)(2,1)} %bitcast.7, s32[1024]{0:T(1024)S(1)} %pad_clamp_fusion), kind=kCustom, calls=%fused_computation.1 | custom fusion | bytes 6291712 | tf_op jit(solution)/shard_map/gather | solution.py:63
  358.2 4.0 pad_maximum_fusion
  362.3 30.1 %while.15 = (s32[]{:T(128)}, bf16[512,768]{1,0:T(8,128)(2,1)S(1)}, pred[2560]{0:T(1024)(128)(4,1)S(1)}, bf16[512,768]{1,0:T(8,128)(2,1)S(1)}, bf16[2560,768]{1,0...) while((s32[]{:T(128)}, bf16[512,768]{1,0:T(8,128)(2,1)S(1)}, ...), condition=%wide.region_8.9_spmd, body=%wide.region_5.8_spmd.sunk | while | flops 680393728 | bytes 17317012 | solution.py:102
  362.3 2.1 fusion.38
  364.4 0.8 fusion.39
  365.2 2.0 fusion.40
  367.3 2.1 fusion.38
  369.4 0.8 fusion.39
  370.2 2.0 fusion.40
  372.3 2.1 fusion.38
  374.4 0.8 fusion.39
  375.2 2.0 fusion.40
  377.3 2.1 fusion.38
  379.4 0.8 fusion.39
  380.3 2.0 fusion.40
  382.3 2.1 fusion.38
  384.5 0.8 fusion.39
  385.3 2.0 fusion.40
  387.4 2.1 fusion.38
  389.5 0.8 fusion.39
  390.3 2.0 fusion.40
  392.4 6.4 %convolution_convert_fusion = bf16[512,3072]{1,0:T(8,128)(2,1)} fusion(bf16[512,768]{1,0:T(8,128)(2,1)S(1)} %get-tuple-element.161, bf16[768,3072]{1,0:T(8,128)(2,1)} %param.19), kind=kOutput, calls=%fused_computation.22 | convolution fusion | flops 2417491968 | bytes 8650752 | tf_op jit(solution)/shard_map/dot_general | solution.py:106
  398.8 37.6 %reduce-scatter.2.cloned.1.call-done = bf16[128,3072]{1,0:T(8,128)(2,1)} async-done(((bf16[512,3072]{1,0:T(8,128)(2,1)}), bf16[128,3072]{1,0:T(8,128)(2,1)}) %reduce-scatter.2.cloned.1.call-update) | async-done | bytes 786448 | tf_op jit(solution)/shard_map/reduce_scatter | solution.py:105
  (24 shorter events, 0.3 us)
Async XLA Ops:
  6.5 13.0 %copy-start = (bf16[24,32,768]{2,1,0:T(8,128)(2,1)S(1)}, bf16[24,32,768]{2,1,0:T(8,128)(2,1)}, u32[]{:S(2)}) copy-start(bf16[24,32,768]{2,1,0:T(8,128)(2,1)} %param.15) | copy-start | bytes 3538948
  8.7 19.2 %all-to-all-start.3 = ((bf16[128,4,768]{2,0,1:T(8,128)(2,1)}), bf16[128,4,768]{2,0,1:T(8,128)(2,1)S(1)}, u32[]{:S(2)}, u32[]{:S(2)}) async-start(bf16[128,4,768]{2,0,1:T(8,128)(2,1)} %bitcast.52), calls=%async_computation.3 | async-start | bytes 1572864 | tf_op jit(solution)/shard_map/all_to_all | solution.py:48
  19.5 3.6 copy-start.2
  23.1 3.8 copy-start.3
  27.9 14.2 %all-to-all-start.1 = ((bf16[128,4,768]{2,0,1:T(8,128)(2,1)}), bf16[128,4,768]{2,0,1:T(8,128)(2,1)S(1)}, u32[]{:S(2)}, u32[]{:S(2)}) async-start(bf16[128,4,768]{2,0,1:T(8,128)(2,1)} %bitcast.53), calls=%async_computation.1 | async-start | bytes 1572864 | tf_op jit(solution)/shard_map/all_to_all | solution.py:47
  198.2 6.3 %copy-start.4 = (bf16[128,3072]{1,0:T(8,128)(2,1)S(1)}, bf16[128,3072]{1,0:T(8,128)(2,1)}, u32[]{:S(2)}) copy-start(bf16[128,3072]{1,0:T(8,128)(2,1)} %param.11) | copy-start | bytes 2359300
  198.2 147.0 %all-to-all-start.2 = ((bf16[64,2,32,768]{3,2,1,0:T(8,128)(2,1)}), bf16[64,2,32,768]{3,2,1,0:T(8,128)(2,1)}, u32[]{:S(2)}, u32[]{:S(2)}) async-start(bf16[64,2,32,768]{3,2,1,0:T(8,128)(2,1)} %get-tuple-element.180), calls=%async_computation.2 | async-start | bytes 12582912 | tf_op jit(solution)/shard_map/all_to_all | solution.py:51
  345.2 17.0 %all-to-all-start = ((bf16[128,4,768]{2,0,1:T(8,128)(2,1)}), bf16[128,4,768]{2,0,1:T(8,128)(2,1)S(1)}, u32[]{:S(2)}, u32[]{:S(2)}) async-start(bf16[128,4,768]{2,0,1:T(8,128)(2,1)} %bitcast.54), calls=%async_computation | async-start | bytes 1572864 | tf_op jit(solution)/shard_map/all_to_all | solution.py:46
  348.7 87.7 %reduce-scatter.2.cloned.1.call-start = ((), (), s32[]{:S(2)}) async-start(), calls=%async_computation.6 | async-start | bytes 3932160 | tf_op jit(solution)/shard_map/reduce_scatter | solution.py:105
  392.4 44.0 %copy-start.1 = (bf16[24,32,768]{2,1,0:T(8,128)(2,1)S(1)}, bf16[24,32,768]{2,1,0:T(8,128)(2,1)}, u32[]{:S(2)}) copy-start(bf16[24,32,768]{2,1,0:T(8,128)(2,1)} %param.15) | copy-start | bytes 3538948
Sparse Core Ops, SparseCore 0:
  398.9 37.3 reduce-scatter.1
where the time goes:
time: 444 us; the launch traced here: 443 us
  waiting for transfers between devices  172 us (39%)
  blocking collectives  156 us (35%)
  matrix products  31.3 us (7%)
  other arithmetic  29.1 us (7%)
  local copies, waits for them, and re-layouts  22.2 us (5%)
  starting transfers between devices  18.9 us (4%)
  between operations  13.5 us (3%)
    all_to_all x1, blocking collectives, local(): lax.all_to_all(send_values, 'frame', split_axis=0, concat_axis=0, tiled=T...  156 us
    all_to_all x1, waiting for transfers between devices, local(): lax.all_to_all(send_keys, 'frame', split_axis=0, concat_axis=0, tiled=True)  134 us
    reduce_scatter x1, waiting for transfers between devices, local(): lax.psum_scatter(jnp.dot(attn, out_weight, preferred_element_type=jnp.flo...  37.6 us
    dot_general x6, matrix products, attend(): jnp.einsum('qd,kd->qk', query_block, head_cols(all_keys, column), preferr...  12.6 us
    dot_general x6, matrix products, attend(): jnp.dot(expo.astype(jnp.bfloat16), head_cols(all_values, column), preferr...  12.3 us
    select_n x1, other arithmetic, local(): jnp.where(filled, bank_v[slot_row], jnp.zeros((), bank_v.dtype))  9.96 us
  transfers between devices with their start and end apart: 5, of which 2 were waited for; matrix products, arithmetic and copies ran while one was open for 10% of the time, Pallas kernels for 0%

commit v1 on v0

v1 whole, which is shorter than its diff:
```python
import math

import jax
import jax.numpy as jnp
from jax import lax
from jax.experimental import pallas as pl
from jax.experimental.pallas import tpu as pltpu
from jax.sharding import PartitionSpec as P

HEAD_DIM = 128
NX, NY, NZ, NC = 4, 4, 8, 2
PLANE = NY * NC
PAIRS = 3
NEG = -1e30
MESH = pl.DeviceIdType.MESH


def side_units(step):
    return [u for u in range(4) if (4 if (u // 2 + u % 2) % 2 == 0 else 3) >= step]


def kernel(
    rows_ref, bias_ref, q_ref, k_ref, v_ref, bk_ref, bv_ref, w_ref,
    out_ref, wfull_ref,
    qx, kx, vx, bank0, bank1, bank2, qt, rb, lb, home, hlse, mine,
    xq_s, xq_r, xk_s, xk_r, own_sem, bo_sem, w_own, w_s, w_r, wd_s, wd_r,
    a_s, a_r, b_s, b_r, d_s, d_r, g_s, g_r, o_s, o_r, l_s, l_r, t_s, t_r, t_own,
):
    frame = lax.axis_index("frame")
    x = lax.axis_index("head")
    y, z, c = frame // (NZ * NC), (frame // NC) % NZ, frame % NC
    rows = q_ref.shape[0]
    width = qx.shape[1]
    frames = bk_ref.shape[0]
    half = frames // 2
    wrows = w_ref.shape[0]
    whalf = wrows // 2
    banks = (bank0, bank1, bank2)
    factor = math.log2(math.e) / math.sqrt(HEAD_DIM)

    def dev_y(step):
        return ((((y + step + NY) % NY) * NZ + z) * NC + c, x)

    def dev_z(step):
        return ((y * NZ + (z + step + NZ) % NZ) * NC + c, x)

    def dev_x(step):
        return (frame, (x + step) % NX)

    sibling = ((y * NZ + z) * NC + 1 - c, x)

    def lanes(start, size):
        return pl.ds(pl.multiple_of(start, HEAD_DIM), size)

    def remote(src, dst, s, r, dev):
        return pltpu.make_async_remote_copy(
            src_ref=src, dst_ref=dst, send_sem=s, recv_sem=r, device_id=dev, device_id_type=MESH
        )

    my_rows = pl.ds(pl.multiple_of(x * rows, rows), rows)

    def x_query(p, dx):
        peer = (x + dx) % NX
        return remote(
            q_ref.at[:, lanes(peer * width + p * 256, 256)],
            qx.at[my_rows, pl.ds(p * 256, 256)],
            xq_s.at[p, dx - 1], xq_r.at[p, dx - 1], dev_x(dx),
        )

    def x_keys(kv, dx):
        peer = (x + dx) % NX
        src, dst = ((k_ref, kx), (v_ref, vx))[kv]
        return remote(
            src.at[:, lanes(peer * width, width)], dst.at[my_rows, :],
            xk_s.at[kv, dx - 1], xk_r.at[kv, dx - 1], dev_x(dx),
        )

    def own_rows(i):
        src, dst = ((q_ref, qx), (k_ref, kx), (v_ref, vx))[i]
        return pltpu.make_async_copy(
            src.at[:, lanes(x * width, width)], dst.at[my_rows, :], own_sem.at[i]
        )

    def own_bank(kv, p):
        return pltpu.make_async_copy(
            (bk_ref, bv_ref)[kv].at[:, :, cols(p)], block(kv, y, p), bo_sem.at[p, kv]
        )

    def cols(p):
        return pl.ds(p * 256, 256)

    def block(kv, yy, p):
        return banks[p].at[kv, pl.ds(((yy + NY) % NY * NC + c) * frames, frames)]

    def half_block(kv, yy, which, p):
        start = ((yy + NY) % NY * NC + c) * frames + which * half
        return banks[p].at[kv, pl.ds(start, half)]

    def bank_a(p, kv, d):
        return remote(
            (bk_ref, bv_ref)[kv].at[:, :, cols(p)], block(kv, y, p),
            a_s.at[p, kv, d], a_r.at[p, kv, d], dev_y(1 - 2 * d),
        )

    def bank_b(p, kv, d):
        view = half_block(kv, y - (1 - 2 * d), d, p)
        return remote(view, view, b_s.at[p, kv, d], b_r.at[p, kv, d], dev_y(1 - 2 * d))

    def bank_d(p, kv, t):
        if t == 0:
            src, dst = (bk_ref, bv_ref)[kv].at[:, :, cols(p)], block(kv, y, p)
        elif t <= 2:
            src = dst = block(kv, y - (1 - 2 * (t - 1)), p)
        else:
            src = dst = half_block(kv, y + 2, t - 3, p)
        return remote(src, dst, d_s.at[p, kv, t], d_r.at[p, kv, t], sibling)

    def ag(s, k, h):
        before = 0 if k == 1 else s * 4 + k - 1
        return remote(
            qt.at[before, h], qt.at[s * 4 + k, h], g_s.at[s, k, h], g_r.at[s, k, h], dev_z(2 * s - 1)
        )

    def back(s, k, h):
        return (
            remote(rb.at[s, k, h], rb.at[s, k - 1, h], o_s.at[s, k, h], o_r.at[s, k - 1, h], dev_z(1 - 2 * s)),
            remote(lb.at[s, k, h], lb.at[s, k - 1, h], l_s.at[s, k, h], l_r.at[s, k - 1, h], dev_z(1 - 2 * s)),
        )

    def w_x(dx):
        return remote(
            w_ref.at[pl.ds(c * whalf, whalf)], wfull_ref.at[pl.ds(x * wrows + c * whalf, whalf)],
            w_s.at[dx - 1], w_r.at[dx - 1], dev_x(dx),
        )

    def w_d(dx):
        view = wfull_ref.at[pl.ds((x - dx + NX) % NX * wrows + c * whalf, whalf)]
        return remote(view, view, wd_s.at[dx - 1], wd_r.at[dx - 1], sibling)

    def w_mine():
        return pltpu.make_async_copy(w_ref, wfull_ref.at[pl.ds(x * wrows, wrows)], w_own)

    def attn_x(p, dx):
        peer = (x + dx) % NX
        return remote(
            mine.at[pl.ds(pl.multiple_of(peer * rows, rows), rows), cols(p)],
            out_ref.at[:, lanes(x * width + p * 256, 256)],
            t_s.at[p, dx - 1], t_r.at[p, dx - 1], dev_x(dx),
        )

    def attn_own(p):
        return pltpu.make_async_copy(
            mine.at[my_rows, cols(p)], out_ref.at[:, lanes(x * width + p * 256, 256)], t_own.at[p]
        )

    def softmax(keys, values, queries, biases):
        scores = jnp.dot(keys, queries, preferred_element_type=jnp.float32) * factor
        if biases is not None:
            step = scores.shape[0] // len(biases)
            scores = jnp.concatenate(
                [scores[i * step : (i + 1) * step] + b for i, b in enumerate(biases)], axis=0
            )
        top = jnp.max(scores, axis=0, keepdims=True)
        expo = jnp.exp2(scores - top)
        total = jnp.sum(expo, axis=0, keepdims=True)
        numer = lax.dot_general(
            values, expo.astype(jnp.bfloat16), (((0,), (0,)), ((), ())),
            preferred_element_type=jnp.float32,
        )
        return numer / total, top + jnp.log2(total)

    def partial(p, odd, index):
        bank, h = banks[p], 2 * p + odd
        here = lanes(odd * HEAD_DIM, HEAD_DIM)
        picked = [rows_ref[index, i] for i in range(2 * PLANE)]
        keys = jnp.concatenate([bank[0, r, :, here] for r in picked], axis=0)
        values = jnp.concatenate([bank[1, r, :, here] for r in picked], axis=0)
        biases = [bias_ref[index, i] for i in range(2 * PLANE)]
        return softmax(keys, values, qt[index, h], biases)

    def merge(a, b):
        (oa, la), (ob, lb_) = a, b
        top = jnp.maximum(la, lb_)
        wa, wb = jnp.exp2(la - top), jnp.exp2(lb_ - top)
        total = wa + wb
        return oa * (wa / total) + ob * (wb / total), top + jnp.log2(total)

    def put(s, k, h, part):
        rb[s, k, h] = part[0].astype(jnp.bfloat16)
        for i in range(4):
            lb[s, k, h, i : i + 1, :] = part[1][:, i * 128 : (i + 1) * 128]

    def get(s, k, h):
        lse = jnp.concatenate([lb[s, k, h, i : i + 1, :] for i in range(4)], axis=1)
        return rb[s, k, h].astype(jnp.float32), lse

    def ag_step(p, k):
        for u in side_units(k):
            s, h = u // 2, 2 * p + u % 2
            if k > 1:
                ag(s, k - 1, h).wait_recv()
            ag(s, k, h).start()

    def ag_end(p):
        for u in range(4):
            s, h = u // 2, 2 * p + u % 2
            ag(s, 4 if (u // 2 + u % 2) % 2 == 0 else 3, h).wait_recv()

    def rs_step(p, j):
        units, stride = (4, 1) if j < 3 else (2, 3)

        def unit(i, carry):
            u = i * stride
            s = u // 2
            odd = u % 2
            h = 2 * p + odd
            k = 4 - (s + odd) % 2 - j
            part = partial(p, odd, s * 4 + k)
            if j:
                for copy in back(s, k + 1, h):
                    copy.wait_recv()
                part = merge(get(s, k, h), part)
            put(s, k, h, part)
            for copy in back(s, k, h):
                copy.start()
            return carry

        lax.fori_loop(0, units, unit, 0)

    def home_part(p):
        def one(i, carry):
            h = 2 * p + i
            here = lanes(h * HEAD_DIM, HEAD_DIM)
            part = merge(partial(p, i, 0), softmax(kx[:, here], vx[:, here], qt[0, h], None))
            home[h] = part[0]
            hlse[h] = part[1]
            return carry

        lax.fori_loop(0, 2, one, 0)

    def finish(p):
        def one(i, carry):
            h = 2 * p + i
            here = lanes(h * HEAD_DIM, HEAD_DIM)
            part = (home[h], hlse[h])
            for s in range(2):
                for copy in back(s, 1, h):
                    copy.wait_recv()
                part = merge(part, get(s, 0, h))
            mine[:, here] = jnp.transpose(part[0]).astype(jnp.bfloat16)
            return carry

        lax.fori_loop(0, 2, one, 0)
        for dx in range(1, NX):
            attn_x(p, dx).start()
        attn_own(p).start()

    def bank_start(p):
        for kv in range(2):
            for d in range(2):
                bank_a(p, kv, d).start()
            bank_d(p, kv, 0).start()

    def bank_pass(p):
        for kv in range(2):
            for d in range(2):
                bank_a(p, kv, d).wait_recv()
                bank_b(p, kv, d).start()
                bank_d(p, kv, 1 + d).start()

    def bank_last(p):
        for kv in range(2):
            for d in range(2):
                bank_b(p, kv, d).wait_recv()
                bank_d(p, kv, 3 + d).start()

    def bank_end(p):
        for kv in range(2):
            own_bank(kv, p).wait()
            for t in range(5):
                bank_d(p, kv, t).wait_recv()

    def load_queries(p):
        for dx in range(1, NX):
            x_query(p, dx).wait_recv()
        for h in (2 * p, 2 * p + 1):
            part = qx[:, h * HEAD_DIM : (h + 1) * HEAD_DIM]
            qt[0, h] = jnp.transpose(part.astype(jnp.float32)).astype(jnp.bfloat16)

    for i in range(3):
        own_rows(i).start()
    for p in range(PAIRS):
        for kv in range(2):
            own_bank(kv, p).start()
    w_mine().start()
    barrier = pltpu.get_barrier_semaphore()
    for dev in (dev_x(1), dev_x(2), dev_x(3), sibling, dev_y(1), dev_y(-1), dev_z(1), dev_z(-1)):
        pl.semaphore_signal(barrier, inc=1, device_id=dev, device_id_type=MESH)
    pl.semaphore_wait(barrier, 8)

    for p in range(PAIRS):
        for dx in range(1, NX):
            x_query(p, dx).start()
    bank_start(0)
    for kv in range(2):
        for dx in range(1, NX):
            x_keys(kv, dx).start()
    own_rows(0).wait()
    load_queries(0)
    ag_step(0, 1)
    load_queries(1)
    ag_step(1, 1)
    load_queries(2)
    for dx in range(1, NX):
        w_x(dx).start()
    ag_step(0, 2)
    ag_step(1, 2)
    bank_pass(0)
    bank_start(1)
    ag_step(0, 3)
    ag_step(1, 3)
    bank_last(0)
    ag_step(0, 4)
    ag_step(1, 4)
    ag_step(2, 1)
    bank_end(0)
    ag_end(0)
    rs_step(0, 0)
    ag_step(2, 2)
    bank_pass(1)
    bank_start(2)
    rs_step(0, 1)
    ag_step(2, 3)
    for i in (1, 2):
        own_rows(i).wait()
    for kv in range(2):
        for dx in range(1, NX):
            x_keys(kv, dx).wait_recv()
    home_part(0)
    bank_last(1)
    rs_step(0, 2)
    ag_step(2, 4)
    bank_end(1)
    ag_end(1)
    rs_step(1, 0)
    rs_step(0, 3)
    bank_pass(2)
    ag_end(2)
    home_part(1)
    rs_step(1, 1)
    bank_last(2)
    bank_end(2)
    rs_step(2, 0)
    finish(0)
    rs_step(1, 2)
    rs_step(2, 1)
    home_part(2)
    rs_step(1, 3)
    rs_step(2, 2)
    for dx in range(1, NX):
        w_x(dx).wait_recv()
        w_d(dx).start()
    rs_step(2, 3)
    finish(1)
    finish(2)

    for p in range(PAIRS):
        for dx in range(1, NX):
            x_query(p, dx).wait_send()
            attn_x(p, dx).wait()
        attn_own(p).wait()
        for kv in range(2):
            for d in range(2):
                bank_a(p, kv, d).wait_send()
                bank_b(p, kv, d).wait_send()
            for t in range(5):
                bank_d(p, kv, t).wait_send()
        for k in range(1, 5):
            for u in side_units(k):
                s, h = u // 2, 2 * p + u % 2
                ag(s, k, h).wait_send()
                for copy in back(s, k, h):
                    copy.wait_send()
    for dx in range(1, NX):
        for kv in range(2):
            x_keys(kv, dx).wait_send()
        w_x(dx).wait_send()
        w_d(dx).wait()
    w_mine().wait()


def plan(frame_slot, picks, counts, per_device):
    frame = lax.axis_index("frame")
    y, z, c = frame // (NZ * NC), (frame // NC) % NZ, frame % NC
    longest = picks.shape[1]
    offsets = jnp.array([0, 1, 2, 3, 4, -1, -2, -3, -4], jnp.int32)
    spans = (y * NZ + (z + offsets + NZ) % NZ) * NC + c
    listed = picks[spans]
    number = counts[spans]
    table = jnp.arange(frame_slot.shape[0], dtype=jnp.int32)
    hits = listed[:, :, None] == table[None, None, :]
    bank_rows = jnp.sum(jnp.where(hits, frame_slot[None, None, :], 0), axis=2)
    position = jnp.arange(longest, dtype=jnp.int32)
    owner = bank_rows // per_device
    here = (position[None, :] < number[:, None]) & ((owner // NC) % NZ == z)
    earlier = here[:, None, :] & (position[None, None, :] < position[None, :, None])
    rank = jnp.sum(earlier.astype(jnp.int32), axis=2)
    local = (owner // (NZ * NC) * NC + owner % NC) * per_device + bank_rows % per_device
    slots = jnp.arange(2 * PLANE, dtype=jnp.int32)
    chosen = here[:, None, :] & (rank[:, None, :] == slots[None, :, None])
    rows = jnp.sum(jnp.where(chosen, local[:, None, :], 0), axis=2)
    bias = jnp.where(jnp.any(chosen, axis=2), 0.0, NEG).astype(jnp.float32)
    return rows, bias


def local(span_q, span_k, span_v, bank_k, bank_v, frame_slot, picks, counts, out_weight):
    rows, bias = plan(frame_slot, picks, counts, bank_k.shape[0])
    width = bank_k.shape[2]
    heads = width // HEAD_DIM
    span_rows = span_q.shape[0] * NX
    model = span_q.shape[1]
    bf, dma = jnp.bfloat16, pltpu.SemaphoreType.DMA
    smem = pl.BlockSpec(memory_space=pltpu.SMEM)
    hbm = pl.BlockSpec(memory_space=pl.ANY)
    attn, weight = pl.pallas_call(
        kernel,
        out_shape=(
            jax.ShapeDtypeStruct((span_q.shape[0], model), bf),
            jax.ShapeDtypeStruct((model, out_weight.shape[1]), bf),
        ),
        in_specs=[smem, smem] + [hbm] * 6,
        out_specs=(pl.BlockSpec(memory_space=pltpu.VMEM), hbm),
        scratch_shapes=[
            pltpu.VMEM((span_rows, width), bf),
            pltpu.VMEM((span_rows, width), bf),
            pltpu.VMEM((span_rows, width), bf),
            *[pltpu.VMEM((2, PLANE * bank_k.shape[0], bank_k.shape[1], 256), bf)] * PAIRS,
            pltpu.VMEM((9, heads, HEAD_DIM, span_rows), bf),
            pltpu.VMEM((2, 5, heads, HEAD_DIM, span_rows), bf),
            pltpu.VMEM((2, 5, heads, 4, 128), jnp.float32),
            pltpu.VMEM((heads, HEAD_DIM, span_rows), jnp.float32),
            pltpu.VMEM((heads, 1, span_rows), jnp.float32),
            pltpu.VMEM((span_rows, width), bf),
            dma((PAIRS, NX - 1)), dma((PAIRS, NX - 1)),
            dma((2, NX - 1)), dma((2, NX - 1)),
            dma((3,)), dma((PAIRS, 2)), dma(()),
            dma((NX - 1,)), dma((NX - 1,)), dma((NX - 1,)), dma((NX - 1,)),
            dma((PAIRS, 2, 2)), dma((PAIRS, 2, 2)),
            dma((PAIRS, 2, 2)), dma((PAIRS, 2, 2)),
            dma((PAIRS, 2, 5)), dma((PAIRS, 2, 5)),
            dma((2, 5, heads)), dma((2, 5, heads)),
            dma((2, 5, heads)), dma((2, 5, heads)),
            dma((2, 5, heads)), dma((2, 5, heads)),
            dma((PAIRS, NX - 1)), dma((PAIRS, NX - 1)), dma((PAIRS,)),
        ],
        compiler_params=pltpu.CompilerParams(
            collective_id=0, has_side_effects=True, vmem_limit_bytes=60 * 2**20
        ),
    )(rows, bias, span_q, span_k, span_v, bank_k, bank_v, out_weight)
    return jnp.dot(attn, weight, preferred_element_type=jnp.float32).astype(bf)


def solution(mesh):
    placed = (
        P(("frame", "head"), None),
        P(("frame", "head"), None),
        P(("frame", "head"), None),
        P("frame", None, "head"),
        P("frame", None, "head"),
        P(),
        P(),
        P(),
        P("head", None),
    )
    return jax.shard_map(
        local, mesh=mesh, in_specs=placed, out_specs=P(("frame", "head"), None), check_vma=False
    )
```

time: 444 us -> 171 us (0.39)
  waiting for transfers between devices: 172 us -> 0 us
  blocking collectives: 156 us -> 0 us
  Pallas kernels: 0 us -> 153 us
  other arithmetic: 29.1 us -> 4.08 us
  matrix products: 31.3 us -> 10.1 us
  local copies, waits for them, and re-layouts: 22.2 us -> 1.88 us
  starting transfers between devices: 18.9 us -> 0 us
  between operations: 13.5 us -> 0.03 us
    all_to_all x1 -> x0, blocking collectives: 156 us -> none  [local(): lax.all_to_all(send_values, 'frame', split_axis=0, concat_axis=0, tiled=T...]
    pallas_call x0 -> x1, Pallas kernels: none -> 153 us  [local(): pl.pallas_call(kernel, out_shape=(jax.ShapeDtypeStruct((span_q.shape[0],...]
    all_to_all x4 -> x0, waiting for transfers between devices: 134 us -> none  [the longest x1 134 us: local(): lax.all_to_all(send_keys, 'frame', split_axis=0, concat_axis=0, tiled=True)]
    reduce_scatter x1 -> x0, waiting for transfers between devices: 37.6 us -> none  [local(): lax.psum_scatter(jnp.dot(attn, out_weight, preferred_element_type=jnp.flo...]
    dot_general x13 -> x1, matrix products: 31.3 us -> 10.1 us  [local(): return jnp.dot(attn, weight, preferred_element_type=jnp.float32).astype(bf)]
    all_to_all x4 -> x0, starting transfers between devices: 18.7 us -> none  [the longest x1 6.11 us: local(): lax.all_to_all(send_keys, 'frame', split_axis=0, concat_axis=0, tiled=True)]
    gather x4 -> x2, local copies, waits for them, and re-layouts: 17.6 us -> 1.88 us  [the longest x1 1.32 us: plan(): number = counts[spans]]
    select_n x4 -> x2, other arithmetic: 10 us -> 1.28 us  [the longest x1 0.68 us: plan(): number = counts[spans]]
  transfers between devices with their start and end apart: 5 -> 0, of which waited for: 2 -> 0; matrix products, arithmetic and copies ran while one was open for 10% -> 0% of each run, Pallas kernels for 0% -> 0%
where the time goes in v1:
time: 171 us; the launch traced here: 169 us
  Pallas kernels  153 us (89%)
  matrix products  10.1 us (6%)
  other arithmetic  4.08 us (2%)
  local copies, waits for them, and re-layouts  1.88 us (1%)
    pallas_call x1, Pallas kernels, local(): pl.pallas_call(kernel, out_shape=(jax.ShapeDtypeStruct((span_q.shape[0],...  153 us
    dot_general x1, matrix products, local(): return jnp.dot(attn, weight, preferred_element_type=jnp.float32).astype(bf)  10.1 us

profile of v1, /device:TPU:1, one launch (start us, length us, event | category | flops | bytes accessed | tf_op | source)
XLA Modules:
  0.0 169.5 jit_solution(10139588617340665770)
XLA Ops:
  0.0 0.0 copy-start
  0.0 0.7 compare_select_fusion
  0.7 1.3 gather_fusion
  2.0 0.0 copy-done
  2.0 0.6 gather_fusion.1
  2.6 1.3 select_reduce_fusion
  3.9 0.1 fusion.11
  4.0 0.2 convert_reduce_fusion
  4.3 0.9 select_reduce_fusion.1.rows_ref
  5.1 0.3 fusion.1
  5.4 0.6 broadcast_select_fusion.bias_ref
  6.0 153.4 %shard_map.100 = (bf16[128,3072]{1,0:T(8,128)(2,1)}, bf16[3072,3072]{1,0:T(8,128)(2,1)}) custom-call(s32[9,16]{1,0:T(8,128)} %select_reduce_fusion.1.rows_ref, f32[9,16]{1,0:T(8,128)} %broadcast_select_fusion.bias_ref, bf16[128,3072]{1,0:T(8,128)(2,1)} %q_ref.1, bf16[128,3072]{1,0:T(8,128)(2,1)} %k_ref.1, bf16[128,3072]{1,0:T(8,128)(2,1)} %v_ref.1, ...), custom_call_target="tpu_custom_call" | custom-call | tf_op jit(solution)/shard_map/pallas_call | solution.py:425
  159.4 10.1 %convolution_convert_fusion = bf16[128,3072]{1,0:T(8,128)(2,1)} fusion(bf16[128,3072]{1,0:T(8,128)(2,1)} %get-tuple-element.7, bf16[3072,3072]{1,0:T(8,128)(2,1)} %get-tuple-element.8), kind=kOutput, calls=%fused_computation.2 | convolution fusion | flops 2416312320 | bytes 20447232 | tf_op jit(solution)/shard_map/dot_general | solution.py:460
  (3 shorter events, 0.0 us)
Async XLA Ops:
  0.0 2.0 %copy-start = (s32[64,64]{1,0:T(8,128)S(1)}, s32[64,64]{1,0:T(8,128)}, u32[]{:S(2)}) copy-start(s32[64,64]{1,0:T(8,128)} %param.16) | copy-start | bytes 49156

commit v2 on v1

--- a/solution.py
+++ b/solution.py
@@ -21,10 +21,11 @@
 
 def kernel(
     rows_ref, bias_ref, q_ref, k_ref, v_ref, bk_ref, bv_ref, w_ref,
-    out_ref, wfull_ref,
-    qx, kx, vx, bank0, bank1, bank2, qt, rb, lb, home, hlse, mine,
-    xq_s, xq_r, xk_s, xk_r, own_sem, bo_sem, w_own, w_s, w_r, wd_s, wd_r,
-    a_s, a_r, b_s, b_r, d_s, d_r, g_s, g_r, o_s, o_r, l_s, l_r, t_s, t_r, t_own,
+    out_ref,
+    qx, kx, vx, bank0, bank1, bank2, qt, rb, lb, home, hlse,
+    arrived, weight, acc,
+    xq_s, xq_r, xk_s, xk_r, own_sem, bo_sem, w_s, w_r, wf_s, wf_r, wd_s, wd_r,
+    a_s, a_r, b_s, b_r, d_s, d_r, g_s, g_r, o_s, o_r, l_s, l_r, t_s, t_r, t_own, w_own,
 ):
     frame = lax.axis_index("frame")
     x = lax.axis_index("head")
@@ -35,6 +36,7 @@
     half = frames // 2
     wrows = w_ref.shape[0]
     whalf = wrows // 2
+    mine = qx
     banks = (bank0, bank1, bank2)
     factor = math.log2(math.e) / math.sqrt(HEAD_DIM)
 
@@ -127,31 +129,39 @@
             remote(lb.at[s, k, h], lb.at[s, k - 1, h], l_s.at[s, k, h], l_r.at[s, k - 1, h], dev_z(1 - 2 * s)),
         )
 
-    def w_x(dx):
+    def w_rows(xx, which, part=None):
+        size = whalf if part is None else whalf // 2
+        start = (xx + NX) % NX * wrows + which * whalf + (0 if part is None else part * size)
+        return weight.at[pl.ds(pl.multiple_of(start, whalf // 2), size)]
+
+    def w_x(d):
         return remote(
-            w_ref.at[pl.ds(c * whalf, whalf)], wfull_ref.at[pl.ds(x * wrows + c * whalf, whalf)],
-            w_s.at[dx - 1], w_r.at[dx - 1], dev_x(dx),
-        )
-
-    def w_d(dx):
-        view = wfull_ref.at[pl.ds((x - dx + NX) % NX * wrows + c * whalf, whalf)]
-        return remote(view, view, wd_s.at[dx - 1], wd_r.at[dx - 1], sibling)
-
-    def w_mine():
-        return pltpu.make_async_copy(w_ref, wfull_ref.at[pl.ds(x * wrows, wrows)], w_own)
+            w_ref.at[pl.ds(c * whalf, whalf)], w_rows(x, c), w_s.at[d], w_r.at[d], dev_x(1 if d == 0 else NX - 1)
+        )
+
+    def w_f(d):
+        view = w_rows(x - (1 - 2 * d), c, d)
+        return remote(view, view, wf_s.at[d], wf_r.at[d], dev_x(1 if d == 0 else NX - 1))
+
+    def w_d(t):
+        view = w_rows(x - (1 - 2 * t), c) if t < 2 else w_rows(x + 2, c)
+        return remote(view, view, wd_s.at[t], wd_r.at[t], sibling)
 
     def attn_x(p, dx):
         peer = (x + dx) % NX
         return remote(
             mine.at[pl.ds(pl.multiple_of(peer * rows, rows), rows), cols(p)],
-            out_ref.at[:, lanes(x * width + p * 256, 256)],
+            arrived.at[:, lanes(x * width + p * 256, 256)],
             t_s.at[p, dx - 1], t_r.at[p, dx - 1], dev_x(dx),
         )
 
     def attn_own(p):
         return pltpu.make_async_copy(
-            mine.at[my_rows, cols(p)], out_ref.at[:, lanes(x * width + p * 256, 256)], t_own.at[p]
-        )
+            mine.at[my_rows, cols(p)], arrived.at[:, lanes(x * width + p * 256, 256)], t_own.at[p]
+        )
+
+    def w_mine():
+        return pltpu.make_async_copy(w_ref, weight.at[pl.ds(pl.multiple_of(x * wrows, wrows), wrows)], w_own)
 
     def softmax(keys, values, queries, biases):
         scores = jnp.dot(keys, queries, preferred_element_type=jnp.float32) * factor
@@ -169,13 +179,13 @@
         )
         return numer / total, top + jnp.log2(total)
 
-    def partial(p, odd, index):
-        bank, h = banks[p], 2 * p + odd
+    def partial(p, odd, index, away):
+        bank, h, where = banks[p], 2 * p + odd, (z + away + NZ) % NZ
         here = lanes(odd * HEAD_DIM, HEAD_DIM)
-        picked = [rows_ref[index, i] for i in range(2 * PLANE)]
+        picked = [rows_ref[where, i] for i in range(2 * PLANE)]
         keys = jnp.concatenate([bank[0, r, :, here] for r in picked], axis=0)
         values = jnp.concatenate([bank[1, r, :, here] for r in picked], axis=0)
-        biases = [bias_ref[index, i] for i in range(2 * PLANE)]
+        biases = [bias_ref[where, i] for i in range(2 * PLANE)]
         return softmax(keys, values, qt[index, h], biases)
 
     def merge(a, b):
@@ -215,7 +225,7 @@
             odd = u % 2
             h = 2 * p + odd
             k = 4 - (s + odd) % 2 - j
-            part = partial(p, odd, s * 4 + k)
+            part = partial(p, odd, s * 4 + k, k - 2 * s * k)
             if j:
                 for copy in back(s, k + 1, h):
                     copy.wait_recv()
@@ -231,7 +241,7 @@
         def one(i, carry):
             h = 2 * p + i
             here = lanes(h * HEAD_DIM, HEAD_DIM)
-            part = merge(partial(p, i, 0), softmax(kx[:, here], vx[:, here], qt[0, h], None))
+            part = merge(partial(p, i, 0, 0), softmax(kx[:, here], vx[:, here], qt[0, h], None))
             home[h] = part[0]
             hlse[h] = part[1]
             return carry
@@ -255,6 +265,41 @@
             attn_x(p, dx).start()
         attn_own(p).start()
 
+    def w_ready():
+        w_mine().wait()
+        for t in range(3):
+            w_d(t).wait_recv()
+
+    def w_pass():
+        for d in range(2):
+            w_x(d).wait_recv()
+            w_f(d).start()
+            w_d(d).start()
+
+    def w_last():
+        for d in range(2):
+            w_f(d).wait_recv()
+        w_d(2).start()
+
+    def project(p):
+        for dx in range(1, NX):
+            attn_x(p, dx).wait_recv()
+        attn_own(p).wait()
+
+        def columns(i, carry):
+            here = pl.ds(pl.multiple_of(i * 512, 512), 512)
+            part = acc[:, here] if p else 0.0
+            for xx in range(NX):
+                deep = pl.ds(xx * width + p * 256, 256)
+                part = part + jnp.dot(arrived[:, deep], weight[deep, here], preferred_element_type=jnp.float32)
+            if p == PAIRS - 1:
+                out_ref[:, here] = part.astype(jnp.bfloat16)
+            else:
+                acc[:, here] = part
+            return carry
+
+        lax.fori_loop(0, out_ref.shape[1] // 512, columns, 0)
+
     def bank_start(p):
         for kv in range(2):
             for d in range(2):
@@ -292,7 +337,6 @@
     for p in range(PAIRS):
         for kv in range(2):
             own_bank(kv, p).start()
-    w_mine().start()
     barrier = pltpu.get_barrier_semaphore()
     for dev in (dev_x(1), dev_x(2), dev_x(3), sibling, dev_y(1), dev_y(-1), dev_z(1), dev_z(-1)):
         pl.semaphore_signal(barrier, inc=1, device_id=dev, device_id_type=MESH)
@@ -302,17 +346,18 @@
         for dx in range(1, NX):
             x_query(p, dx).start()
     bank_start(0)
-    for kv in range(2):
-        for dx in range(1, NX):
-            x_keys(kv, dx).start()
     own_rows(0).wait()
     load_queries(0)
     ag_step(0, 1)
     load_queries(1)
     ag_step(1, 1)
     load_queries(2)
-    for dx in range(1, NX):
-        w_x(dx).start()
+    for kv in range(2):
+        for dx in range(1, NX):
+            x_keys(kv, dx).start()
+    w_mine().start()
+    for d in range(2):
+        w_x(d).start()
     ag_step(0, 2)
     ag_step(1, 2)
     bank_pass(0)
@@ -348,6 +393,7 @@
     ag_end(2)
     home_part(1)
     rs_step(1, 1)
+    w_pass()
     bank_last(2)
     bank_end(2)
     rs_step(2, 0)
@@ -356,19 +402,20 @@
     rs_step(2, 1)
     home_part(2)
     rs_step(1, 3)
+    w_last()
     rs_step(2, 2)
-    for dx in range(1, NX):
-        w_x(dx).wait_recv()
-        w_d(dx).start()
+    finish(1)
+    w_ready()
     rs_step(2, 3)
-    finish(1)
+    project(0)
+    project(1)
     finish(2)
+    project(2)
 
     for p in range(PAIRS):
         for dx in range(1, NX):
             x_query(p, dx).wait_send()
-            attn_x(p, dx).wait()
-        attn_own(p).wait()
+            attn_x(p, dx).wait_send()
         for kv in range(2):
             for d in range(2):
                 bank_a(p, kv, d).wait_send()
@@ -384,19 +431,20 @@
     for dx in range(1, NX):
         for kv in range(2):
             x_keys(kv, dx).wait_send()
-        w_x(dx).wait_send()
-        w_d(dx).wait()
-    w_mine().wait()
+    for d in range(2):
+        w_x(d).wait_send()
+        w_f(d).wait_send()
+    for t in range(3):
+        w_d(t).wait_send()
 
 
 def plan(frame_slot, picks, counts, per_device):
     frame = lax.axis_index("frame")
     y, z, c = frame // (NZ * NC), (frame // NC) % NZ, frame % NC
     longest = picks.shape[1]
-    offsets = jnp.array([0, 1, 2, 3, 4, -1, -2, -3, -4], jnp.int32)
-    spans = (y * NZ + (z + offsets + NZ) % NZ) * NC + c
-    listed = picks[spans]
-    number = counts[spans]
+    listed = lax.dynamic_slice(picks.reshape(NY, NZ, NC, longest), (y, 0, c, 0), (1, NZ, 1, longest))
+    listed = listed.reshape(NZ, longest)
+    number = lax.dynamic_slice(counts.reshape(NY, NZ, NC), (y, 0, c), (1, NZ, 1)).reshape(NZ)
     table = jnp.arange(frame_slot.shape[0], dtype=jnp.int32)
     hits = listed[:, :, None] == table[None, None, :]
     bank_rows = jnp.sum(jnp.where(hits, frame_slot[None, None, :], 0), axis=2)
@@ -422,14 +470,11 @@
     bf, dma = jnp.bfloat16, pltpu.SemaphoreType.DMA
     smem = pl.BlockSpec(memory_space=pltpu.SMEM)
     hbm = pl.BlockSpec(memory_space=pl.ANY)
-    attn, weight = pl.pallas_call(
+    return pl.pallas_call(
         kernel,
-        out_shape=(
-            jax.ShapeDtypeStruct((span_q.shape[0], model), bf),
-            jax.ShapeDtypeStruct((model, out_weight.shape[1]), bf),
-        ),
+        out_shape=jax.ShapeDtypeStruct((span_q.shape[0], out_weight.shape[1]), bf),
         in_specs=[smem, smem] + [hbm] * 6,
-        out_specs=(pl.BlockSpec(memory_space=pltpu.VMEM), hbm),
+        out_specs=pl.BlockSpec(memory_space=pltpu.VMEM),
         scratch_shapes=[
             pltpu.VMEM((span_rows, width), bf),
             pltpu.VMEM((span_rows, width), bf),
@@ -440,24 +485,25 @@
             pltpu.VMEM((2, 5, heads, 4, 128), jnp.float32),
             pltpu.VMEM((heads, HEAD_DIM, span_rows), jnp.float32),
             pltpu.VMEM((heads, 1, span_rows), jnp.float32),
-            pltpu.VMEM((span_rows, width), bf),
+            pltpu.VMEM((span_q.shape[0], model), bf),
+            pltpu.VMEM((model, out_weight.shape[1]), bf),
+            pltpu.VMEM((span_q.shape[0], out_weight.shape[1]), jnp.float32),
             dma((PAIRS, NX - 1)), dma((PAIRS, NX - 1)),
             dma((2, NX - 1)), dma((2, NX - 1)),
-            dma((3,)), dma((PAIRS, 2)), dma(()),
-            dma((NX - 1,)), dma((NX - 1,)), dma((NX - 1,)), dma((NX - 1,)),
+            dma((3,)), dma((PAIRS, 2)),
+            dma((2,)), dma((2,)), dma((2,)), dma((2,)), dma((3,)), dma((3,)),
             dma((PAIRS, 2, 2)), dma((PAIRS, 2, 2)),
             dma((PAIRS, 2, 2)), dma((PAIRS, 2, 2)),
             dma((PAIRS, 2, 5)), dma((PAIRS, 2, 5)),
             dma((2, 5, heads)), dma((2, 5, heads)),
             dma((2, 5, heads)), dma((2, 5, heads)),
             dma((2, 5, heads)), dma((2, 5, heads)),
-            dma((PAIRS, NX - 1)), dma((PAIRS, NX - 1)), dma((PAIRS,)),
+            dma((PAIRS, NX - 1)), dma((PAIRS, NX - 1)), dma((PAIRS,)), dma(()),
         ],
         compiler_params=pltpu.CompilerParams(
-            collective_id=0, has_side_effects=True, vmem_limit_bytes=60 * 2**20
+            collective_id=0, has_side_effects=True, vmem_limit_bytes=63 * 2**20
         ),
     )(rows, bias, span_q, span_k, span_v, bank_k, bank_v, out_weight)
-    return jnp.dot(attn, weight, preferred_element_type=jnp.float32).astype(bf)
 
 
 def solution(mesh):

time: 171 us -> 160 us (0.936)
  matrix products: 10.1 us -> 0 us
  local copies, waits for them, and re-layouts: 1.88 us -> 3.77 us
    dot_general x1 -> x0, matrix products: 10.1 us -> none  [local(): return jnp.dot(attn, weight, preferred_element_type=jnp.float32).astype(bf)]
    unnamed x2 -> x3, local copies, waits for them, and re-layouts: 0.01 us -> 2.82 us
    gather x2 -> x0, local copies, waits for them, and re-layouts: 1.88 us -> none  [the longest x1 1.32 us: plan(): number = counts[spans]]
where the time goes in v2:
time: 160 us; the launch traced here: 159 us
  Pallas kernels  152 us (95%)
  local copies, waits for them, and re-layouts  3.77 us (2%)
  other arithmetic  3.23 us (2%)
    pallas_call x1, Pallas kernels, local(): pl.pallas_call(kernel, out_shape=jax.ShapeDtypeStruct((span_q.shape[0], o...  152 us

profile of v2, /device:TPU:1, one launch (start us, length us, event | category | flops | bytes accessed | tf_op | source)
XLA Modules:
  0.0 159.2 jit_solution(16169746561735985073)
XLA Ops:
  0.0 0.0 copy-start
  0.0 0.8 copy-done
  0.8 1.3 select_reduce_fusion
  2.1 0.8 reshape.113
  2.8 0.2 dynamic-slice_reduce_fusion
  3.0 0.1 fusion.11
  3.1 0.2 convert_reduce_fusion
  3.3 0.8 select_reduce_fusion.1.rows_ref
  4.1 0.2 fusion.1
  4.4 0.6 broadcast_select_fusion.bias_ref
  5.0 152.2 %shard_map.91 = bf16[128,3072]{1,0:T(8,128)(2,1)} custom-call(s32[8,16]{1,0:T(8,128)} %select_reduce_fusion.1.rows_ref, f32[8,16]{1,0:T(8,128)} %broadcast_select_fusion.bias_ref, bf16[128,3072]{1,0:T(8,128)(2,1)} %q_ref.1, bf16[128,3072]{1,0:T(8,128)(2,1)} %k_ref.1, bf16[128,3072]{1,0:T(8,128)(2,1)} %v_ref.1, bf16[24,32,768]{2,1,0:T(8,128)(2,1)} %bk_ref.1, ...), custom_call_target="tpu_custom_call" | custom-call | tf_op jit(solution)/shard_map/pallas_call | solution.py:473
  157.2 2.1 %copy.11 = bf16[128,3072]{1,0:T(8,128)(2,1)} copy(bf16[128,3072]{1,0:T(8,128)(2,1)} %shard_map.91) | data formatting | bytes 1572864
  (3 shorter events, 0.0 us)
Async XLA Ops:
  0.0 0.8 copy-start

commit v3 on v2

--- a/solution.py
+++ b/solution.py
@@ -20,12 +20,12 @@
 
 
 def kernel(
-    rows_ref, bias_ref, q_ref, k_ref, v_ref, bk_ref, bv_ref, w_ref,
+    picks_ref, counts_ref, slot_ref, q_ref, k_ref, v_ref, bk_ref, bv_ref, w_ref,
     out_ref,
     qx, kx, vx, bank0, bank1, bank2, qt, rb, lb, home, hlse,
-    arrived, weight, acc,
+    arrived, weight, acc, table_v, table,
     xq_s, xq_r, xk_s, xk_r, own_sem, bo_sem, w_s, w_r, wf_s, wf_r, wd_s, wd_r,
-    a_s, a_r, b_s, b_r, d_s, d_r, g_s, g_r, o_s, o_r, l_s, l_r, t_s, t_r, t_own, w_own,
+    a_s, a_r, b_s, b_r, d_s, d_r, g_s, g_r, o_s, o_r, l_s, l_r, t_s, t_r, t_own, w_own, table_sem,
 ):
     frame = lax.axis_index("frame")
     x = lax.axis_index("head")
@@ -182,10 +182,11 @@
     def partial(p, odd, index, away):
         bank, h, where = banks[p], 2 * p + odd, (z + away + NZ) % NZ
         here = lanes(odd * HEAD_DIM, HEAD_DIM)
-        picked = [rows_ref[where, i] for i in range(2 * PLANE)]
+        listed = [table[where, i] for i in range(2 * PLANE)]
+        picked = [jnp.maximum(r, 0) for r in listed]
         keys = jnp.concatenate([bank[0, r, :, here] for r in picked], axis=0)
         values = jnp.concatenate([bank[1, r, :, here] for r in picked], axis=0)
-        biases = [bias_ref[where, i] for i in range(2 * PLANE)]
+        biases = [jnp.where(r < 0, NEG, 0.0) for r in listed]
         return softmax(keys, values, qt[index, h], biases)
 
     def merge(a, b):
@@ -203,6 +204,40 @@
     def get(s, k, h):
         lse = jnp.concatenate([lb[s, k, h, i : i + 1, :] for i in range(4)], axis=1)
         return rb[s, k, h].astype(jnp.float32), lse
+
+    def plan():
+        first = y * NZ * NC + c
+        listed = picks_ref[pl.ds(first, NZ, stride=NC), :]
+        span = lax.broadcasted_iota(jnp.int32, listed.shape, 0)
+        position = lax.broadcasted_iota(jnp.int32, listed.shape, 1)
+        number = jnp.zeros(listed.shape, jnp.int32)
+        for i in range(NZ):
+            number = jnp.where(span == i, counts_ref[first + i * NC], number)
+
+        def look(i, found):
+            for j in range(8):
+                t = i * 8 + j
+                found = jnp.where(listed == t, slot_ref[t], found)
+            return found
+
+        found = lax.fori_loop(0, slot_ref.shape[0] // 8, look, jnp.zeros(listed.shape, jnp.int32))
+        magic = -(-65536 // frames)
+        owner = (found * magic) >> 16
+        here = (position < number) & (((owner >> 1) & (NZ - 1)) == z)
+        holder = ((owner >> 4) << 1) + (owner & 1)
+        place = holder * frames + found - owner * frames
+        lane = lax.broadcasted_iota(jnp.int32, table_v.shape, 1)
+        out = jnp.full(table_v.shape, -1, jnp.int32)
+        for m in range(PLANE):
+            mine_here = here & (holder == m)
+            high = jnp.max(jnp.where(mine_here, place, -1), axis=1, keepdims=True)
+            low = jnp.min(jnp.where(mine_here, place, 1 << 20), axis=1, keepdims=True)
+            out = jnp.where(lane == 2 * m, high, out)
+            out = jnp.where(lane == 2 * m + 1, jnp.where(low < high, low, -1), out)
+        table_v[...] = out
+        copy = pltpu.make_async_copy(table_v, table, table_sem)
+        copy.start()
+        copy.wait()
 
     def ag_step(p, k):
         for u in side_units(k):
@@ -358,6 +393,7 @@
     w_mine().start()
     for d in range(2):
         w_x(d).start()
+    plan()
     ag_step(0, 2)
     ag_step(1, 2)
     bank_pass(0)
@@ -405,11 +441,11 @@
     w_last()
     rs_step(2, 2)
     finish(1)
+    rs_step(2, 3)
+    finish(2)
     w_ready()
-    rs_step(2, 3)
     project(0)
     project(1)
-    finish(2)
     project(2)
 
     for p in range(PAIRS):
@@ -438,31 +474,7 @@
         w_d(t).wait_send()
 
 
-def plan(frame_slot, picks, counts, per_device):
-    frame = lax.axis_index("frame")
-    y, z, c = frame // (NZ * NC), (frame // NC) % NZ, frame % NC
-    longest = picks.shape[1]
-    listed = lax.dynamic_slice(picks.reshape(NY, NZ, NC, longest), (y, 0, c, 0), (1, NZ, 1, longest))
-    listed = listed.reshape(NZ, longest)
-    number = lax.dynamic_slice(counts.reshape(NY, NZ, NC), (y, 0, c), (1, NZ, 1)).reshape(NZ)
-    table = jnp.arange(frame_slot.shape[0], dtype=jnp.int32)
-    hits = listed[:, :, None] == table[None, None, :]
-    bank_rows = jnp.sum(jnp.where(hits, frame_slot[None, None, :], 0), axis=2)
-    position = jnp.arange(longest, dtype=jnp.int32)
-    owner = bank_rows // per_device
-    here = (position[None, :] < number[:, None]) & ((owner // NC) % NZ == z)
-    earlier = here[:, None, :] & (position[None, None, :] < position[None, :, None])
-    rank = jnp.sum(earlier.astype(jnp.int32), axis=2)
-    local = (owner // (NZ * NC) * NC + owner % NC) * per_device + bank_rows % per_device
-    slots = jnp.arange(2 * PLANE, dtype=jnp.int32)
-    chosen = here[:, None, :] & (rank[:, None, :] == slots[None, :, None])
-    rows = jnp.sum(jnp.where(chosen, local[:, None, :], 0), axis=2)
-    bias = jnp.where(jnp.any(chosen, axis=2), 0.0, NEG).astype(jnp.float32)
-    return rows, bias
-
-
 def local(span_q, span_k, span_v, bank_k, bank_v, frame_slot, picks, counts, out_weight):
-    rows, bias = plan(frame_slot, picks, counts, bank_k.shape[0])
     width = bank_k.shape[2]
     heads = width // HEAD_DIM
     span_rows = span_q.shape[0] * NX
@@ -473,7 +485,7 @@
     return pl.pallas_call(
         kernel,
         out_shape=jax.ShapeDtypeStruct((span_q.shape[0], out_weight.shape[1]), bf),
-        in_specs=[smem, smem] + [hbm] * 6,
+        in_specs=[pl.BlockSpec(memory_space=pltpu.VMEM), smem, smem] + [hbm] * 6,
         out_specs=pl.BlockSpec(memory_space=pltpu.VMEM),
         scratch_shapes=[
             pltpu.VMEM((span_rows, width), bf),
@@ -488,6 +500,8 @@
             pltpu.VMEM((span_q.shape[0], model), bf),
             pltpu.VMEM((model, out_weight.shape[1]), bf),
             pltpu.VMEM((span_q.shape[0], out_weight.shape[1]), jnp.float32),
+            pltpu.VMEM((NZ, 128), jnp.int32),
+            pltpu.SMEM((NZ, 128), jnp.int32),
             dma((PAIRS, NX - 1)), dma((PAIRS, NX - 1)),
             dma((2, NX - 1)), dma((2, NX - 1)),
             dma((3,)), dma((PAIRS, 2)),
@@ -498,12 +512,12 @@
             dma((2, 5, heads)), dma((2, 5, heads)),
             dma((2, 5, heads)), dma((2, 5, heads)),
             dma((2, 5, heads)), dma((2, 5, heads)),
-            dma((PAIRS, NX - 1)), dma((PAIRS, NX - 1)), dma((PAIRS,)), dma(()),
+            dma((PAIRS, NX - 1)), dma((PAIRS, NX - 1)), dma((PAIRS,)), dma(()), dma(()),
         ],
         compiler_params=pltpu.CompilerParams(
             collective_id=0, has_side_effects=True, vmem_limit_bytes=63 * 2**20
         ),
-    )(rows, bias, span_q, span_k, span_v, bank_k, bank_v, out_weight)
+    )(picks, counts, frame_slot, span_q, span_k, span_v, bank_k, bank_v, out_weight)
 
 
 def solution(mesh):

time: 160 us -> 154 us (0.963)
  other arithmetic: 3.23 us -> 0 us
  local copies, waits for them, and re-layouts: 3.77 us -> 2.06 us
    reduce_sum x3 -> x0, other arithmetic: 2.3 us -> none  [the longest x1 1.27 us: plan(): bank_rows = jnp.sum(jnp.where(hits, frame_slot[None, None, :], 0), axis=2)]
where the time goes in v3:
time: 154 us
  Pallas kernels  151 us (98%)
  local copies, waits for them, and re-layouts  2.06 us (1%)
    pallas_call x1, Pallas kernels, local(): pl.pallas_call(kernel, out_shape=jax.ShapeDtypeStruct((span_q.shape[0], o...  151 us

profile of v3, /device:TPU:1, one launch (start us, length us, event | category | flops | bytes accessed | tf_op | source)
XLA Modules:
  0.0 153.5 jit_solution(11606503272729127252)
XLA Ops:
  0.0 151.4 %shard_map.91 = bf16[128,3072]{1,0:T(8,128)(2,1)} custom-call(s32[64,64]{1,0:T(8,128)} %picks_ref.1, s32[64]{0:T(128)} %counts_ref.1, s32[1536]{0:T(1024)} %slot_ref.1, bf16[128,3072]{1,0:T(8,128)(2,1)} %q_ref.1, bf16[128,3072]{1,0:T(8,128)(2,1)} %k_ref.1, bf16[128,3072]{1,0:T(8,128)(2,1)} %v_ref.1, bf16[24,32,768]{2,1,0:T(8,128)(2,1)} %bk_ref.1, ...), custom_call_target="tpu_custom_call" | custom-call | tf_op jit(solution)/shard_map/pallas_call | solution.py:485
  151.4 2.1 %copy.11 = bf16[128,3072]{1,0:T(8,128)(2,1)} copy(bf16[128,3072]{1,0:T(8,128)(2,1)} %shard_map.91) | data formatting | bytes 1572864

commit v4 on v3

--- a/solution.py
+++ b/solution.py
@@ -425,11 +425,11 @@
     ag_end(1)
     rs_step(1, 0)
     rs_step(0, 3)
+    w_pass()
     bank_pass(2)
     ag_end(2)
     home_part(1)
     rs_step(1, 1)
-    w_pass()
     bank_last(2)
     bank_end(2)
     rs_step(2, 0)
@@ -437,8 +437,8 @@
     rs_step(1, 2)
     rs_step(2, 1)
     home_part(2)
+    w_last()
     rs_step(1, 3)
-    w_last()
     rs_step(2, 2)
     finish(1)
     rs_step(2, 3)

time: 154 us -> 151 us (0.981)
  Pallas kernels: 151 us -> 149 us
    pallas_call x1, Pallas kernels: 151 us -> 149 us  [local(): pl.pallas_call(kernel, out_shape=jax.ShapeDtypeStruct((span_q.shape[0], o...]
where the time goes in v4:
time: 151 us
  Pallas kernels  149 us (99%)
  local copies, waits for them, and re-layouts  2.06 us (1%)
    pallas_call x1, Pallas kernels, local(): pl.pallas_call(kernel, out_shape=jax.ShapeDtypeStruct((span_q.shape[0], o...  149 us

profile of v4, /device:TPU:1, one launch (start us, length us, event | category | flops | bytes accessed | tf_op | source)
XLA Modules:
  0.0 151.3 jit_solution(5525625140414338633)
XLA Ops:
  0.0 149.2 %shard_map.91 = bf16[128,3072]{1,0:T(8,128)(2,1)} custom-call(s32[64,64]{1,0:T(8,128)} %picks_ref.1, s32[64]{0:T(128)} %counts_ref.1, s32[1536]{0:T(1024)} %slot_ref.1, bf16[128,3072]{1,0:T(8,128)(2,1)} %q_ref.1, bf16[128,3072]{1,0:T(8,128)(2,1)} %k_ref.1, bf16[128,3072]{1,0:T(8,128)(2,1)} %v_ref.1, bf16[24,32,768]{2,1,0:T(8,128)(2,1)} %bk_ref.1, ...), custom_call_target="tpu_custom_call" | custom-call | tf_op jit(solution)/shard_map/pallas_call | solution.py:485
  149.2 2.1 %copy.11 = bf16[128,3072]{1,0:T(8,128)(2,1)} copy(bf16[128,3072]{1,0:T(8,128)(2,1)} %shard_map.91) | data formatting | bytes 1572864
